TPU v7x, 32 devices: a whole 2x2x4 slice. The times are simulated.
32 devices in a mesh: row: 4 (over y, x), col: 8 (over z, core).
Axes of the slice: x: 2, y: 2, z: 4, core: 2. Of those that a mesh axis runs over, the one named last changes fastest.
Arguments:
- trailing_grad: bfloat16 [4, 8, 768, 24576], P(None, 'col', None, 'row'), may hold values from -6 to 6
- panel: bfloat16 [24576, 512], P(('row', 'col')), may hold values from -0.0390625 to 0.0390625
- panel_grad: float32 [24576, 512], P(('row', 'col')), may hold values from -6 to 6
- diag_factor: float32 [512, 512], replicated, may hold values from -2 to 2, as said below
- diag_grad: float32 [512, 512], replicated, may hold values from -6 to 6
Outputs:
- panel_adj: float32 [24576, 512], P(('row', 'col'))
- diag_adj: float32 [512, 512], replicated
Inputs may be any that keep to these rules, and one draw needn't show every extreme that they name: `diag_factor`: lower triangular with zeros above the diagonal; diagonal entries between 1 and 2.
All inputs are finite; a program needn't handle non-finite values.
Results may differ from a plain program's by a relative error of at most 0.0003.
Values may be sent and summed in bfloat16 or wider, within the bound.
A program may use at most 128 MiB of HBM per device.

v0:
```python
import jax
import jax.numpy as jnp
from jax import lax
from jax.sharding import PartitionSpec as P


def halve_lower(matrix):
    rows = lax.broadcasted_iota(jnp.int32, matrix.shape, 0)
    cols = lax.broadcasted_iota(jnp.int32, matrix.shape, 1)
    keep = jnp.where(rows > cols, 1.0, jnp.where(rows == cols, 0.5, 0.0)).astype(jnp.float32)
    return matrix * keep


def keep_lower(matrix):
    rows = lax.broadcasted_iota(jnp.int32, matrix.shape, 0)
    cols = lax.broadcasted_iota(jnp.int32, matrix.shape, 1)
    return jnp.where(rows >= cols, matrix, 0.0)


def right_solve(left, lower):
    right = jax.scipy.linalg.solve_triangular(lower, left.T, lower=True, trans=1).T
    return 0.5 * (right + right.T)


def on_device(trailing_grad, panel, panel_grad, diag_factor, diag_grad):
    local_flip = trailing_grad.reshape(-1, trailing_grad.shape[3])
    lower = jnp.tril(diag_factor)
    col_panel = lax.all_gather(panel, "row", axis=0, tiled=True)
    row_panel = lax.all_gather(panel, "col", axis=0, tiled=True)
    block = local_flip
    direct = lax.psum_scatter(
        lax.dot_general(
            block, col_panel, (((0,), (0,)), ((), ())), preferred_element_type=jnp.float32
        ),
        "col",
        scatter_dimension=0,
        tiled=True,
    )
    block = local_flip
    transposed = lax.psum_scatter(
        jnp.dot(block, row_panel, preferred_element_type=jnp.float32),
        "row",
        scatter_dimension=0,
        tiled=True,
    )
    reduced = panel_grad - direct - transposed
    panel_adj = jax.scipy.linalg.solve_triangular(lower, reduced.T, lower=True, trans=1).T
    contrib = lax.dot_general(
        panel_adj,
        panel.astype(jnp.float32),
        (((0,), (0,)), ((), ())),
        precision=lax.Precision.HIGHEST,
    )
    diag_new = diag_grad - lax.psum(contrib, ("row", "col"))
    inner = halve_lower(jnp.dot(lower.T, keep_lower(diag_new), precision=lax.Precision.HIGHEST))
    left = jax.scipy.linalg.solve_triangular(lower, inner, lower=True, trans=1)
    return (panel_adj, right_solve(left, lower))


def solution(mesh):
    in_specs = (
        P(None, "col", None, "row"),
        P(("row", "col"), None),
        P(("row", "col"), None),
        P(),
        P(),
    )
    out_specs = (P(("row", "col"), None), P())
    return jax.shard_map(
        on_device, mesh=mesh, in_specs=in_specs, out_specs=out_specs, check_vma=False
    )
```

profile of v0, /device:TPU:0, one launch (start us, length us, event | category | flops | bytes accessed | tf_op | source)
XLA Modules:
  0.0 489.1 jit_solution(2284740775558172705)
XLA Ops:
  7.2 0.7 all-gather.5.cloned.1.call-update
  7.9 0.7 all-gather.3.cloned.1.call-update
  8.7 68.4 %all-gather.5.cloned.1.call-done = bf16[6144,512]{1,0:T(8,128)(2,1)} async-done(((bf16[768,512]{1,0:T(8,128)(2,1)}), bf16[6144,512]{1,0:T(8,128)(2,1)}) %all-gather.5.cloned.1.call-update) | async-done | bytes 6291472 | tf_op jit(solution)/shard_map/all_gather | solution.py:29
  77.1 26.8 %fusion.67 = f32[3072,512]{1,0:T(8,128)} fusion(bf16[3072,6144]{1,0:T(8,128)(2,1)} %bitcast.70, bf16[6144,512]{1,0:T(8,128)(2,1)} %all-gather.5.cloned.1.call-done), kind=kOutput, calls=%fused_computation.91 | convolution fusion | flops 19327352832 | bytes 50331648 | tf_op jit(solution)/shard_map/dot_general | solution.py:41
  103.9 17.5 %all-gather.3.cloned.1.call-done = bf16[3072,512]{1,0:T(8,128)(2,1)} async-done(((bf16[768,512]{1,0:T(8,128)(2,1)}), bf16[3072,512]{1,0:T(8,128)(2,1)}) %all-gather.3.cloned.1.call-update) | async-done | bytes 3145744 | tf_op jit(solution)/shard_map/all_gather | solution.py:28
  121.4 27.7 %fusion.66 = f32[6144,512]{1,0:T(8,128)} fusion(bf16[3072,6144]{1,0:T(8,128)(2,1)} %bitcast.71, bf16[3072,512]{1,0:T(8,128)(2,1)} %all-gather.3.cloned.1.call-done), kind=kOutput, calls=%fused_computation.90 | convolution fusion | flops 19327352832 | bytes 53477376 | tf_op jit(solution)/shard_map/dot_general | solution.py:32
  149.2 1.1 copy-done.6
  150.5 8.0 %while.5 = (s32[]{:T(128)}, f32[512,512]{1,0:T(8,128)S(1)}, s32[4,2]{0,1:T(2,128)S(1)}, f32[4,128,128]{2,1,0:T(8,128)S(1)}, s32[]{:T(128)}) while((s32[]{:T(128)}, f32[512,512]{1,0:T(8,128)S(1)}, s32[4,2]{0,1:T(2,128)S(1)}, f32[4,128,128]{2,1,0:T(8,128)S(1)}, s32[]{:T(128)}) %tuple.32), condition=%wide.while_cond.1, body=%wide.while_body.1.sunk | while | flops 2 | bytes 131181 | solution.py:47
  150.6 0.5 fusion.86
  151.1 1.4 bitcast_dynamic-update-slice_fusion.2
  152.6 0.5 fusion.86
  153.1 1.3 bitcast_dynamic-update-slice_fusion.2
  154.6 0.5 fusion.86
  155.1 1.3 bitcast_dynamic-update-slice_fusion.2
  156.5 0.5 fusion.86
  157.1 1.3 bitcast_dynamic-update-slice_fusion.2
  158.5 39.5 %custom-call.7 = f32[4,128,128]{1,2,0:T(8,128)S(1)} custom-call(f32[4,128,128]{2,1,0:T(8,128)S(1)} %get-tuple-element.18), custom_call_target="InvertDiagBlocksLowerTriangular" | custom-call | tf_op jit(solution)/shard_map/jit(_solve_triangular)/triangular_solve | solution.py:47
  198.0 127.9 %reduce-scatter.3.cloned.1.call-done = f32[768,512]{1,0:T(8,128)} async-done(((f32[6144,512]{1,0:T(8,128)}), f32[768,512]{1,0:T(8,128)}) %reduce-scatter.3.cloned.1.call-update) | async-done | bytes 1572880 | tf_op jit(solution)/shard_map/reduce_scatter | solution.py:31
  325.9 2.9 subtract_bitcast_fusion
  328.8 0.5 fusion.33
  329.3 0.8 convolution_subtract_fusion.1
  330.1 0.5 fusion.53
  330.6 1.4 convolution_subtract_fusion.2
  332.0 0.5 fusion.50
  332.5 2.1 convolution_subtract_fusion
  334.7 1.2 fusion.47
  335.9 3.4 fusion.10
  339.3 1.2 fusion.11
  340.5 1.6 copy.8
  342.2 126.4 %all-reduce.2.cloned.1.call-done = f32[512,512]{1,0:T(8,128)} async-done(((f32[512,512]{1,0:T(8,128)}), f32[512,512]{1,0:T(8,128)}) %all-reduce.2.cloned.1.call-update) | async-done | bytes 1048592 | tf_op jit(solution)/shard_map/psum | solution.py:54
  468.6 3.7 convolution_multiply_fusion
  472.3 0.4 fusion.37
  472.7 0.4 convolution_subtract_fusion.6
  473.1 0.4 fusion.52
  473.5 0.5 convolution_subtract_fusion.5
  474.0 0.4 fusion.49
  474.3 0.9 convolution_subtract_fusion.8
  475.2 0.4 fusion.45
  475.7 0.4 fusion.35
  476.1 0.6 convolution_subtract_fusion.4
  476.7 0.4 fusion.51
  477.1 1.0 convolution_subtract_fusion.3
  478.1 0.4 fusion.48
  478.5 1.5 convolution_subtract_fusion.7
  479.9 0.4 fusion.46
  480.4 0.3 copy.7
  480.8 0.6 copy-done.1
  481.4 1.2 add_multiply_fusion
  (31 shorter events, 0.9 us)
Async XLA Ops:
  7.2 69.9 %all-gather.5.cloned.1.call-start = ((), (), s32[]{:S(2)}) async-start(), calls=%async_computation.4 | async-start | bytes 7077888 | tf_op jit(solution)/shard_map/all_gather | solution.py:29
  7.9 113.5 %all-gather.3.cloned.1.call-start = ((), (), s32[]{:S(2)}) async-start(), calls=%async_computation.2 | async-start | bytes 3932160 | tf_op jit(solution)/shard_map/all_gather | solution.py:28
  8.6 189.3 %reduce-scatter.5.cloned.1.call-start = ((), (), s32[]{:S(2)}) async-start(), calls=%async_computation.5 | async-start | bytes 7864320 | tf_op jit(solution)/shard_map/reduce_scatter | solution.py:40
  103.8 222.1 %reduce-scatter.3.cloned.1.call-start = ((), (), s32[]{:S(2)}) async-start(), calls=%async_computation.3 | async-start | bytes 14155776 | tf_op jit(solution)/shard_map/reduce_scatter | solution.py:31
  149.1 1.2 copy-start.6
  149.1 319.4 %all-reduce.2.cloned.1.call-start = ((), (), s32[]{:S(2)}) async-start(), calls=%async_computation.6 | async-start | bytes 2097152 | tf_op jit(solution)/shard_map/psum | solution.py:54
  198.0 136.7 %copy-start.4 = (f32[4,128,128]{1,2,0:T(8,128)}, f32[4,128,128]{1,2,0:T(8,128)S(1)}, u32[]{:S(2)}) copy-start(f32[4,128,128]{1,2,0:T(8,128)S(1)} %custom-call.7) | copy-start | bytes 786436
  332.5 3.4 copy-start.2
  332.5 3.4 copy-start.3
  342.2 130.1 %copy-start.5 = (f32[4,128,128]{1,2,0:T(8,128)S(1)}, f32[4,128,128]{1,2,0:T(8,128)}, u32[]{:S(2)}) copy-start(f32[4,128,128]{1,2,0:T(8,128)} %copy-done.4) | copy-start | bytes 786436
  478.4 1.9 copy-start
  480.4 1.0 copy-start.1
Sparse Core Ops, SparseCore 0:
  9.6 67.4 all-gather.4
  78.9 42.4 all-gather.2
  124.4 70.1 reduce-scatter.4
  196.8 129.1 reduce-scatter.2
  339.4 129.0 all-reduce.1
where the time goes:
time: 489 us
  waiting for transfers between devices  342 us (70%)
  matrix products  76.4 us (16%)
  other arithmetic  45.1 us (9%)
  between operations  14.1 us (3%)
  local copies, waits for them, and re-layouts  11.6 us (2%)
    reduce_scatter x1, waiting for transfers between devices, on_device(): lax.psum_scatter(lax.dot_general(block, col_panel, (((0,), (0,)), ((), ()...  128 us
    psum x1, waiting for transfers between devices, on_device(): diag_new = diag_grad - lax.psum(contrib, ('row', 'col'))  126 us
    all_gather x1, waiting for transfers between devices, on_device(): row_panel = lax.all_gather(panel, 'col', axis=0, tiled=True)  68.4 us
    another operation x3, other arithmetic, on_device(): jax.scipy.linalg.solve_triangular(lower, reduced.T, lower=True, trans=1)  39.6 us
    dot_general x1, matrix products, on_device(): lax.dot_general(block, col_panel, (((0,), (0,)), ((), ())), preferred_ele...  27.7 us
    dot_general x1, matrix products, on_device(): jnp.dot(block, row_panel, preferred_element_type=jnp.float32)  26.8 us
    all_gather x1, waiting for transfers between devices, on_device(): col_panel = lax.all_gather(panel, 'row', axis=0, tiled=True)  17.5 us
  transfers between devices with their start and end apart: 5, of which 4 were waited for; matrix products, arithmetic and copies ran while one was open for 21% of the time, Pallas kernels for 0%

commit v1 on v0

--- a/solution.py
+++ b/solution.py
@@ -51,7 +51,7 @@
         (((0,), (0,)), ((), ())),
         precision=lax.Precision.HIGHEST,
     )
-    diag_new = diag_grad - lax.psum(contrib, ("row", "col"))
+    diag_new = diag_grad - jnp.sum(lax.all_gather(contrib, ("row", "col")), axis=0)
     inner = halve_lower(jnp.dot(lower.T, keep_lower(diag_new), precision=lax.Precision.HIGHEST))
     left = jax.scipy.linalg.solve_triangular(lower, inner, lower=True, trans=1)
     return (panel_adj, right_solve(left, lower))

time: 489 us -> 565 us (1.16)
  waiting for transfers between devices: 342 us -> 405 us
  other arithmetic: 45.1 us -> 57.4 us
    all_gather x0 -> x1, waiting for transfers between devices: none -> 190 us  [on_device(): lax.all_gather(contrib, ('row', 'col'))]
    psum x1 -> x0, waiting for transfers between devices: 126 us -> none  [on_device(): diag_new = diag_grad - lax.psum(contrib, ('row', 'col'))]
    reduce_sum x0 -> x1, other arithmetic: none -> 12.5 us  [on_device(): jnp.sum(lax.all_gather(contrib, ('row', 'col')), axis=0)]
  transfers between devices with their start and end apart: 5 -> 5, of which waited for: 4 -> 4; matrix products, arithmetic and copies ran while one was open for 21% -> 19% of each run, Pallas kernels for 0% -> 0%
where the time goes in v1:
time: 565 us; the launch traced here: 564 us
  waiting for transfers between devices  405 us (72%)
  matrix products  75.6 us (13%)
  other arithmetic  57.4 us (10%)
  between operations  14.1 us (2%)
  local copies, waits for them, and re-layouts  11.5 us (2%)
    all_gather x1, waiting for transfers between devices, on_device(): lax.all_gather(contrib, ('row', 'col'))  190 us
    reduce_scatter x1, waiting for transfers between devices, on_device(): lax.psum_scatter(lax.dot_general(block, col_panel, (((0,), (0,)), ((), ()...  128 us
    all_gather x1, waiting for transfers between devices, on_device(): row_panel = lax.all_gather(panel, 'col', axis=0, tiled=True)  68.4 us
    another operation x3, other arithmetic, on_device(): jax.scipy.linalg.solve_triangular(lower, reduced.T, lower=True, trans=1)  39.4 us
    dot_general x1, matrix products, on_device(): lax.dot_general(block, col_panel, (((0,), (0,)), ((), ())), preferred_ele...  27.7 us
    dot_general x1, matrix products, on_device(): jnp.dot(block, row_panel, preferred_element_type=jnp.float32)  26.8 us
    all_gather x1, waiting for transfers between devices, on_device(): col_panel = lax.all_gather(panel, 'row', axis=0, tiled=True)  17.5 us
    reduce_sum x1, other arithmetic, on_device(): jnp.sum(lax.all_gather(contrib, ('row', 'col')), axis=0)  12.5 us
  transfers between devices with their start and end apart: 5, of which 4 were waited for; matrix products, arithmetic and copies ran while one was open for 19% of the time, Pallas kernels for 0%

profile of v1, /device:TPU:0, one launch (start us, length us, event | category | flops | bytes accessed | tf_op | source)
XLA Modules:
  0.0 564.4 jit_solution(389542779910302173)
XLA Ops:
  7.2 0.7 all-gather.7.cloned.1.call-update
  7.9 0.7 all-gather.5.cloned.1.call-update
  8.7 68.4 %all-gather.7.cloned.1.call-done = bf16[6144,512]{1,0:T(8,128)(2,1)} async-done(((bf16[768,512]{1,0:T(8,128)(2,1)}), bf16[6144,512]{1,0:T(8,128)(2,1)}) %all-gather.7.cloned.1.call-update) | async-done | bytes 6291472 | tf_op jit(solution)/shard_map/all_gather | solution.py:29
  77.1 26.8 %fusion.67 = f32[3072,512]{1,0:T(8,128)} fusion(bf16[3072,6144]{1,0:T(8,128)(2,1)} %bitcast.72, bf16[6144,512]{1,0:T(8,128)(2,1)} %all-gather.7.cloned.1.call-done), kind=kOutput, calls=%fused_computation.91 | convolution fusion | flops 19327352832 | bytes 50331648 | tf_op jit(solution)/shard_map/dot_general | solution.py:41
  103.9 17.5 %all-gather.5.cloned.1.call-done = bf16[3072,512]{1,0:T(8,128)(2,1)} async-done(((bf16[768,512]{1,0:T(8,128)(2,1)}), bf16[3072,512]{1,0:T(8,128)(2,1)}) %all-gather.5.cloned.1.call-update) | async-done | bytes 3145744 | tf_op jit(solution)/shard_map/all_gather | solution.py:28
  121.4 27.7 %fusion.66 = f32[6144,512]{1,0:T(8,128)} fusion(bf16[3072,6144]{1,0:T(8,128)(2,1)} %bitcast.73, bf16[3072,512]{1,0:T(8,128)(2,1)} %all-gather.5.cloned.1.call-done), kind=kOutput, calls=%fused_computation.90 | convolution fusion | flops 19327352832 | bytes 53477376 | tf_op jit(solution)/shard_map/dot_general | solution.py:32
  149.4 0.9 copy-done.6
  150.5 8.1 %while.5 = (s32[]{:T(128)}, f32[512,512]{1,0:T(8,128)S(1)}, s32[4,2]{0,1:T(2,128)S(1)}, f32[4,128,128]{2,1,0:T(8,128)S(1)}, s32[]{:T(128)}) while((s32[]{:T(128)}, f32[512,512]{1,0:T(8,128)S(1)}, s32[4,2]{0,1:T(2,128)S(1)}, f32[4,128,128]{2,1,0:T(8,128)S(1)}, s32[]{:T(128)}) %tuple.32), condition=%wide.while_cond.1, body=%wide.while_body.1.sunk | while | flops 2 | bytes 131189 | solution.py:47
  150.6 0.5 fusion.86
  151.1 1.4 bitcast_dynamic-update-slice_fusion.2
  152.6 0.5 fusion.86
  153.2 1.4 bitcast_dynamic-update-slice_fusion.2
  154.6 0.5 fusion.86
  155.2 1.4 bitcast_dynamic-update-slice_fusion.2
  156.7 0.5 fusion.86
  157.2 1.4 bitcast_dynamic-update-slice_fusion.2
  158.6 39.3 %custom-call.7 = f32[4,128,128]{1,2,0:T(8,128)S(1)} custom-call(f32[4,128,128]{2,1,0:T(8,128)S(1)} %get-tuple-element.18), custom_call_target="InvertDiagBlocksLowerTriangular" | custom-call | tf_op jit(solution)/shard_map/jit(_solve_triangular)/triangular_solve | solution.py:47
  197.9 128.0 %reduce-scatter.3.cloned.1.call-done = f32[768,512]{1,0:T(8,128)} async-done(((f32[6144,512]{1,0:T(8,128)}), f32[768,512]{1,0:T(8,128)}) %reduce-scatter.3.cloned.1.call-update) | async-done | bytes 1572880 | tf_op jit(solution)/shard_map/reduce_scatter | solution.py:31
  325.9 2.9 subtract_bitcast_fusion
  328.8 0.5 fusion.33
  329.3 0.8 convolution_subtract_fusion.1
  330.1 0.5 fusion.53
  330.6 1.4 convolution_subtract_fusion.2
  332.0 0.5 fusion.50
  332.5 2.1 convolution_subtract_fusion
  334.7 1.2 fusion.47
  335.9 3.4 fusion.10
  339.3 1.2 fusion.11
  340.5 1.6 copy.8
  342.1 190.0 %all-gather.9.cloned.1.call-done = f32[16384,512]{1,0:T(8,128)} async-done(((f32[512,512]{1,0:T(8,128)}), f32[16384,512]{1,0:T(8,128)}) %all-gather.9.cloned.1.call-update) | async-done | bytes 33554448 | tf_op jit(solution)/shard_map/all_gather | solution.py:54
  532.1 12.5 %reduce_sum.9 = f32[512,512]{1,0:T(8,128)S(1)} reduce(f32[32,512,512]{2,1,0:T(8,128)} %bitcast.71, f32[]{:T(128)} %constant.23.clone.1), dimensions={0}, to_apply=%region_2.3 | reduce | flops 8126464 | bytes 34603012 | tf_op jit(solution)/shard_map/reduce_sum | solution.py:54
  544.7 3.1 convolution_multiply_fusion
  547.8 0.4 fusion.37
  548.2 0.4 convolution_subtract_fusion.6
  548.7 0.4 fusion.52
  549.0 0.5 convolution_subtract_fusion.5
  549.5 0.4 fusion.49
  549.9 0.7 convolution_subtract_fusion.8
  550.5 0.4 fusion.45
  551.0 0.4 fusion.35
  551.4 0.6 convolution_subtract_fusion.4
  552.0 0.4 fusion.51
  552.4 1.0 convolution_subtract_fusion.3
  553.4 0.4 fusion.48
  553.8 1.5 convolution_subtract_fusion.7
  555.2 0.4 fusion.46
  556.1 0.6 copy-done.1
  556.7 1.2 add_multiply_fusion
  (34 shorter events, 1.4 us)
Async XLA Ops:
  7.2 69.9 %all-gather.7.cloned.1.call-start = ((), (), s32[]{:S(2)}) async-start(), calls=%async_computation.4 | async-start | bytes 7077888 | tf_op jit(solution)/shard_map/all_gather | solution.py:29
  7.9 113.5 %all-gather.5.cloned.1.call-start = ((), (), s32[]{:S(2)}) async-start(), calls=%async_computation.2 | async-start | bytes 3932160 | tf_op jit(solution)/shard_map/all_gather | solution.py:28
  8.6 189.3 %reduce-scatter.5.cloned.1.call-start = ((), (), s32[]{:S(2)}) async-start(), calls=%async_computation.5 | async-start | bytes 7864320 | tf_op jit(solution)/shard_map/reduce_scatter | solution.py:40
  103.8 222.1 %reduce-scatter.3.cloned.1.call-start = ((), (), s32[]{:S(2)}) async-start(), calls=%async_computation.3 | async-start | bytes 14155776 | tf_op jit(solution)/shard_map/reduce_scatter | solution.py:31
  149.2 1.2 copy-start.6
  149.2 382.9 %all-gather.9.cloned.1.call-start = ((), (), s32[]{:S(2)}) async-start(), calls=%async_computation.6 | async-start | bytes 34603008 | tf_op jit(solution)/shard_map/all_gather | solution.py:54
  197.9 136.7 %copy-start.4 = (f32[4,128,128]{1,2,0:T(8,128)}, f32[4,128,128]{1,2,0:T(8,128)S(1)}, u32[]{:S(2)}) copy-start(f32[4,128,128]{1,2,0:T(8,128)S(1)} %custom-call.7) | copy-start | bytes 786436
  332.5 3.4 copy-start.2
  332.5 3.4 copy-start.3
  532.1 12.6 %copy-start.7 = (f32[512,512]{1,0:T(8,128)S(1)}, f32[512,512]{1,0:T(8,128)}, u32[]{:S(2)}) copy-start(f32[512,512]{1,0:T(8,128)} %param.10) | copy-start | bytes 3145732
  544.7 3.2 copy-start.5
  553.7 1.9 copy-start
  555.7 1.0 copy-start.1
Sparse Core Ops, SparseCore 0:
  9.6 67.4 all-gather.6
  78.9 42.4 all-gather.4
  124.4 70.1 reduce-scatter.4
  196.8 129.1 reduce-scatter.2
  339.4 192.6 all-gather.8
